TPU v7x, 32 devices: a whole 2x2x4 slice. The times are simulated.
32 devices in a mesh: ens: 8 (over y, x, core), lon: 4 (over z).
Axes of the slice: x: 2, y: 2, z: 4, core: 2. Of those that a mesh axis runs over, the one named last changes fastest.
Arguments:
- features: bfloat16 [8, 384, 46080], P('ens', None, 'lon'), may hold values from -6 to 6
- proj_weight: bfloat16 [648, 384], replicated, may hold values from -0.3125 to 0.3125
- basis_vals: float32 [32, 32, 9], replicated, may hold values from -0.375 to 0.375
- row_of: int32 [32, 32], replicated, may hold values from 0 to 31
- col_off: int32 [32, 32], replicated, may hold values from -4 to 4
- observed: float32 [72, 46080], P(None, 'lon'), may hold values from -6 to 6
- lat_weight: float32 [32], replicated, may hold values from 0.3 to 1
Outputs:
- feature_grad: bfloat16 [8, 384, 46080], P('ens', None, 'lon')
- weight_grad: float32 [648, 384], replicated
Inputs may be any that keep to these rules, and one draw needn't show every extreme that they name: row_of names a row of the slab. col_off is a longitude offset in columns.
All inputs are finite; a program needn't handle non-finite values.
Results may differ from a plain program's by a relative error of at most 0.0089.
Values may be sent and summed in bfloat16 or wider, within the bound.
A program may use at most 256 MiB of HBM per device.

v0:
```python
import math
import jax
import jax.numpy as jnp
from jax import lax
from jax.sharding import PartitionSpec as P

O = 72
K = 9
R = 4
LAT = 32
SMOOTH = 0.25


def extended(cells, sides, width):
    for axis, dim in sides:
        count = lax.axis_size(axis)
        head = lax.slice_in_dim(cells, 0, width, axis=dim)
        tail = lax.slice_in_dim(cells, cells.shape[dim] - width, cells.shape[dim], axis=dim)
        cells = jnp.concatenate(
            [
                lax.ppermute(tail, axis, [(i, (i + 1) % count) for i in range(count)]),
                cells,
                lax.ppermute(head, axis, [((i + 1) % count, i) for i in range(count)]),
            ],
            axis=dim,
        )
    return cells


def passed_along(value, axis, steps):
    count = lax.axis_size(axis)
    pairs = [(source, (source + steps) % count) for source in range(count)]
    return lax.ppermute(value, axis, pairs)


def kernel_table(basis_vals, row_of, col_off):
    offsets = jnp.arange(2 * R + 1, dtype=jnp.int32) - R
    row_ids = jnp.arange(LAT, dtype=jnp.int32)
    row_hit = (row_of[:, :, None] == row_ids[None, None, :]).astype(jnp.float32)
    col_hit = (col_off[:, :, None] == offsets[None, None, :]).astype(jnp.float32)
    kernel = jnp.einsum(
        "isk,isr,isd->dkir", basis_vals, row_hit, col_hit, precision=lax.Precision.HIGHEST
    )
    return kernel.astype(jnp.bfloat16)


def smooth_slope(diff):
    return diff / jnp.sqrt(diff * diff + SMOOTH * SMOOTH)


def pair_spread(values, others):

    def add_member(index, total):
        single = lax.dynamic_index_in_dim(others, index, 0, keepdims=True)
        return total + smooth_slope(values - single)

    return lax.fori_loop(0, others.shape[0], add_member, jnp.zeros(values.shape, jnp.float32))


def shards(features, proj_weight, basis_vals, row_of, col_off, observed, lat_weight):
    mem_dev = features.shape[0]
    chan_in = features.shape[1]
    cell_count = features.shape[2]
    lon_dev = cell_count // LAT
    rim_cells = R * LAT
    span = lon_dev * O
    kernel = kernel_table(basis_vals, row_of, col_off)
    weight_three = proj_weight.reshape(K, O, chan_in)
    widened = extended(features, (("lon", 2),), rim_cells)
    widened = widened.reshape(mem_dev, chan_in, lon_dev + 2 * R, LAT)
    projected = jnp.einsum(
        "koc,mcjr->mkrjo", weight_three, widened, preferred_element_type=jnp.float32
    ).astype(jnp.bfloat16)
    projected = projected.reshape(mem_dev, K, LAT, (lon_dev + 2 * R) * O)
    decoded = jnp.zeros((mem_dev, LAT, span), jnp.float32)
    for offset in range(2 * R + 1):
        window = projected[:, :, :, offset * O : offset * O + span]
        decoded = decoded + jnp.einsum(
            "kir,mkrx->mix", kernel[offset], window, preferred_element_type=jnp.float32
        )
    flat_out = decoded.reshape(mem_dev, LAT * span)
    observed_flat = observed.reshape(O, lon_dev, LAT).transpose(2, 1, 0).reshape(LAT * span)
    everyone = lax.all_gather(flat_out, "ens", axis=0, tiled=True)
    total_count = everyone.shape[0]
    spread = pair_spread(flat_out, everyone)
    slopes = smooth_slope(flat_out - observed_flat[None, :]) - spread / (total_count - 1)
    cotangent = (slopes.reshape(mem_dev, LAT, span) * lat_weight[None, :, None]).astype(
        jnp.bfloat16
    )
    padded = jnp.pad(cotangent, ((0, 0), (0, 0), (2 * R * O, 2 * R * O)))
    ext_len = (lon_dev + 2 * R) * O
    stacked = jnp.stack(
        [
            padded[:, :, (2 * R - offset) * O : (2 * R - offset) * O + ext_len]
            for offset in range(2 * R + 1)
        ]
    )
    spread_wide = jnp.einsum("dkir,dmix->mkrx", kernel, stacked, preferred_element_type=jnp.float32)
    left_part = spread_wide[:, :, :, : R * O]
    right_part = spread_wide[:, :, :, (lon_dev + R) * O :]
    from_left = passed_along(right_part.astype(jnp.bfloat16), "lon", 1).astype(right_part.dtype)
    from_right = passed_along(left_part.astype(jnp.bfloat16), "lon", -1).astype(left_part.dtype)
    interior = spread_wide[:, :, :, R * O : (lon_dev + R) * O]
    interior = interior.at[:, :, :, : R * O].add(from_left)
    interior = interior.at[:, :, :, span - R * O :].add(from_right)
    grad_local = interior.astype(jnp.bfloat16).reshape(mem_dev, K, LAT, lon_dev, O)
    feature_grad = jnp.einsum(
        "koc,mkrjo->mcjr", weight_three, grad_local, preferred_element_type=jnp.float32
    ).astype(jnp.bfloat16)
    feature_grad = feature_grad.reshape(mem_dev, chan_in, cell_count)
    feature_cells = features.reshape(mem_dev, chan_in, lon_dev, LAT)
    weight_part = jnp.einsum(
        "mkrjo,mcjr->koc", grad_local, feature_cells, preferred_element_type=jnp.float32
    ).reshape(K * O, chan_in)
    members_all = mem_dev * lax.axis_size("ens")
    columns_all = lon_dev * lax.axis_size("lon")
    weight_grad = lax.psum(weight_part, ("ens", "lon")) / math.sqrt(members_all * columns_all * LAT)
    return (feature_grad, weight_grad)


def solution(mesh):
    in_specs = (P("ens", None, "lon"), P(), P(), P(), P(), P(None, "lon"), P())
    out_specs = (P("ens", None, "lon"), P())
    return jax.shard_map(shards, mesh=mesh, in_specs=in_specs, out_specs=out_specs, check_vma=False)
```

profile of v0, /device:TPU:0, one launch (start us, length us, event | category | flops | bytes accessed | tf_op | source)
XLA Modules:
  0.0 897.1 jit_solution(3145240483996057671)
XLA Ops:
  38.8 24.2 %convert_bitcast_fusion = bf16[1,9,32,368,72]{4,2,1,3,0:T(8,128)(2,1)} fusion(bf16[384,368,32,1]{0,2,3,1:T(8,128)(2,1)} %bitcast.191, bf16[9,72,384,1]{2,1,0,3:T(8,128)(2,1)S(1)} %bitcast.183), kind=kOutput, calls=%fused_computation.21 | convolution fusion | flops 5868122112 | bytes 24803328 | tf_op jit(solution)/shard_map/koc,mcjr->mkrjo/dot_general | solution.py:71
  63.0 23.9 %copy.95 = bf16[1,9,32,368,72]{4,3,2,1,0:T(8,128)(2,1)} copy(bf16[1,9,32,368,72]{4,2,1,3,0:T(8,128)(2,1)} %convert_bitcast_fusion) | data formatting | bytes 30523392 | tf_op jit(solution)/shard_map/convert_element_type | solution.py:73
  86.9 39.8 %reshape.238 = bf16[1,9,32,26496]{3,2,1,0:T(8,128)(2,1)} reshape(bf16[1,9,32,368,72]{4,3,2,1,0:T(8,128)(2,1)} %copy.95) | data formatting | bytes 30523392 | tf_op jit(solution)/shard_map/reshape | solution.py:74
  251.1 95.3 %all-gather.3.cloned.1.call-done = f32[8,1,829440]{2,1,0:T(1,128)} async-done(((f32[1,1,829440]{2,1,0:T(1,128)}), f32[8,1,829440]{2,1,0:T(1,128)}) %all-gather.3.cloned.1.call-update) | async-done | bytes 26542096 | tf_op jit(solution)/shard_map/all_gather | solution.py:83
  346.4 22.3 %copy.152 = f32[8,1,829440]{2,0,1:T(8,128)} copy(f32[8,1,829440]{2,1,0:T(1,128)} %all-gather.3.cloned.1.call-done) | data formatting | bytes 53084160
  368.7 126.8 %while.16 = (s32[]{:T(128)}, f32[1,829440]{1,0:T(1,128)}, f32[8,829440]{1,0:T(8,128)}, f32[1,829440]{1,0:T(1,128)}, s32[]{:T(128)}, /*index=5*/s32[]{:T(128)}) while((s32[]{:T(128)}, f32[1,829440]{1,0:T(1,128)}, f32[8,829440]{1,0:T(8,128)}, f32[1,829440]{1,0:T(1,128)}, s32[]{:T(128)}, /*index=5*/s32[]{:T(128)}) %tuple.65), condition=%wide.region_1.2_spmd.clone, body=%wide.region_0.1_spmd.clone.sunk | while | flops 4976643 | bytes 13271123 | solution.py:57
  368.7 15.1 %fusion.45 = f32[1,829440]{1,0:T(1,128)} fusion(f32[1,829440]{1,0:T(1,128)} %get-tuple-element.182, pred[]{:T(512)S(6)} %compare.15, f32[1,829440]{1,0:T(1,128)} %get-tuple-element.190, f32[8,829440]{1,0:T(8,128)} %get-tuple-element.189, s32[]{:T(128)} %get-tuple-element.181), kind=kLoop, calls=%fused_computation.1.clone.1 | loop fusion | flops 4976640 | bytes 13271045 | tf_op jit(solution)/shard_map/while/body/eval_jaxpr/add | solution.py:55
  383.8 16.0 %fusion.45 = f32[1,829440]{1,0:T(1,128)} fusion(f32[1,829440]{1,0:T(1,128)} %get-tuple-element.182, pred[]{:T(512)S(6)} %compare.15, f32[1,829440]{1,0:T(1,128)} %get-tuple-element.190, f32[8,829440]{1,0:T(8,128)} %get-tuple-element.189, s32[]{:T(128)} %get-tuple-element.181), kind=kLoop, calls=%fused_computation.1.clone.1 | loop fusion | flops 4976640 | bytes 13271045 | tf_op jit(solution)/shard_map/while/body/eval_jaxpr/add | solution.py:55
  399.7 16.0 %fusion.45 = f32[1,829440]{1,0:T(1,128)} fusion(f32[1,829440]{1,0:T(1,128)} %get-tuple-element.182, pred[]{:T(512)S(6)} %compare.15, f32[1,829440]{1,0:T(1,128)} %get-tuple-element.190, f32[8,829440]{1,0:T(8,128)} %get-tuple-element.189, s32[]{:T(128)} %get-tuple-element.181), kind=kLoop, calls=%fused_computation.1.clone.1 | loop fusion | flops 4976640 | bytes 13271045 | tf_op jit(solution)/shard_map/while/body/eval_jaxpr/add | solution.py:55
  415.7 16.0 %fusion.45 = f32[1,829440]{1,0:T(1,128)} fusion(f32[1,829440]{1,0:T(1,128)} %get-tuple-element.182, pred[]{:T(512)S(6)} %compare.15, f32[1,829440]{1,0:T(1,128)} %get-tuple-element.190, f32[8,829440]{1,0:T(8,128)} %get-tuple-element.189, s32[]{:T(128)} %get-tuple-element.181), kind=kLoop, calls=%fused_computation.1.clone.1 | loop fusion | flops 4976640 | bytes 13271045 | tf_op jit(solution)/shard_map/while/body/eval_jaxpr/add | solution.py:55
  431.6 16.0 %fusion.45 = f32[1,829440]{1,0:T(1,128)} fusion(f32[1,829440]{1,0:T(1,128)} %get-tuple-element.182, pred[]{:T(512)S(6)} %compare.15, f32[1,829440]{1,0:T(1,128)} %get-tuple-element.190, f32[8,829440]{1,0:T(8,128)} %get-tuple-element.189, s32[]{:T(128)} %get-tuple-element.181), kind=kLoop, calls=%fused_computation.1.clone.1 | loop fusion | flops 4976640 | bytes 13271045 | tf_op jit(solution)/shard_map/while/body/eval_jaxpr/add | solution.py:55
  447.6 16.0 %fusion.45 = f32[1,829440]{1,0:T(1,128)} fusion(f32[1,829440]{1,0:T(1,128)} %get-tuple-element.182, pred[]{:T(512)S(6)} %compare.15, f32[1,829440]{1,0:T(1,128)} %get-tuple-element.190, f32[8,829440]{1,0:T(8,128)} %get-tuple-element.189, s32[]{:T(128)} %get-tuple-element.181), kind=kLoop, calls=%fused_computation.1.clone.1 | loop fusion | flops 4976640 | bytes 13271045 | tf_op jit(solution)/shard_map/while/body/eval_jaxpr/add | solution.py:55
  463.5 16.0 %fusion.45 = f32[1,829440]{1,0:T(1,128)} fusion(f32[1,829440]{1,0:T(1,128)} %get-tuple-element.182, pred[]{:T(512)S(6)} %compare.15, f32[1,829440]{1,0:T(1,128)} %get-tuple-element.190, f32[8,829440]{1,0:T(8,128)} %get-tuple-element.189, s32[]{:T(128)} %get-tuple-element.181), kind=kLoop, calls=%fused_computation.1.clone.1 | loop fusion | flops 4976640 | bytes 13271045 | tf_op jit(solution)/shard_map/while/body/eval_jaxpr/add | solution.py:55
  479.5 16.0 %fusion.45 = f32[1,829440]{1,0:T(1,128)} fusion(f32[1,829440]{1,0:T(1,128)} %get-tuple-element.182, pred[]{:T(512)S(6)} %compare.15, f32[1,829440]{1,0:T(1,128)} %get-tuple-element.190, f32[8,829440]{1,0:T(8,128)} %get-tuple-element.189, s32[]{:T(128)} %get-tuple-element.181), kind=kLoop, calls=%fused_computation.1.clone.1 | loop fusion | flops 4976640 | bytes 13271045 | tf_op jit(solution)/shard_map/while/body/eval_jaxpr/add | solution.py:55
  495.4 37.4 %subtract_reduce_fusion = f32[829440]{0:T(1024)} fusion(f32[1,829440]{1,0:T(1,128)} %get-tuple-element.105, f32[1,829440]{1,0:T(1,128)} %get-tuple-element.195, f32[1,829440]{1,0:T(1,128)} %broadcast_in_dim_reshape.3), kind=kLoop, calls=%fused_computation.37 | loop fusion | flops 4976640 | bytes 13271040 | tf_op jit(solution)/shard_map/sub | solution.py:86
  554.0 23.7 %fusion.37 = (bf16[1,9,32,26496]{3,2,1,0:T(8,128)(2,1)}, f32[1,9,32,26496]{3,2,1,0:T(8,128)}) fusion(bf16[9,9,32,32]{3,1,0,2:T(8,128)(2,1)S(1)} %copy-done.3, bf16[9,1,32,26496]{3,2,0,1:T(8,128)(2,1)} %bitcast_dynamic-update-slice_fusion.8), kind=kOutput, calls=%fused_computation.83 | convolution fusion | flops 4402999296 | bytes 61212672 | tf_op jit(solution)/shard_map/dkir,dmix->mkrx/dot_general | solution.py:98
  592.8 24.6 %slice.209 = f32[1,9,32,25920]{3,2,1,0:T(8,128)} slice(f32[1,9,32,26496]{3,2,1,0:T(8,128)} %get-tuple-element.149), slice={[0:1], [0:9], [0:32], [288:26208]} | slice | bytes 59719680 | tf_op jit(solution)/shard_map/slice | solution.py:103
  629.5 16.5 %convert_element_type.58 = bf16[1,9,32,25920]{3,2,1,0:T(8,128)(2,1)} convert(f32[1,9,32,25920]{3,2,1,0:T(8,128)} %scatter-add.9) | non-fusion elementwise | flops 7464960 | bytes 44789760 | tf_op jit(solution)/shard_map/convert_element_type | solution.py:106
  646.0 39.2 %reshape.252 = bf16[9,32,360,72]{3,2,1,0:T(8,128)(2,1)} reshape(bf16[1,9,32,25920]{3,2,1,0:T(8,128)(2,1)} %convert_element_type.58) | data formatting | bytes 29859840 | tf_op jit(solution)/shard_map/reshape.105
  685.2 31.7 %copy.119 = bf16[9,72,360,32]{2,3,1,0:T(8,128)(2,1)} copy(bf16[9,72,360,32]{1,2,3,0:T(8,128)(2,1)} %bitcast.185) | data formatting | bytes 29859840 | tf_op jit(solution)/shard_map/mkrjo,mcjr->koc/dot_general | solution.py:112
  716.9 26.0 %copy.121 = bf16[648,360,32]{0,2,1:T(8,128)(2,1)} copy(bf16[648,360,32]{1,2,0:T(8,128)(2,1)} %bitcast.187) | data formatting | bytes 29859840 | tf_op jit(solution)/shard_map/mkrjo,mcjr->koc/dot_general | solution.py:112
  742.9 14.1 %convolution_bitcast_fusion.10 = f32[648,384]{1,0:T(8,128)} fusion(bf16[648,360,32]{0,2,1:T(8,128)(2,1)} %copy.121, bf16[384,360,32]{0,2,1:T(8,128)(2,1)} %bitcast.188), kind=kOutput, calls=%fused_computation.51 | convolution fusion | flops 5733089280 | bytes 24772608 | tf_op jit(solution)/shard_map/mkrjo,mcjr->koc/dot_general | solution.py:112
  757.0 17.2 %fusion.11 = bf16[1,384,360,32]{1,2,3,0:T(8,128)(2,1)} fusion(bf16[9,32,360,72]{3,2,1,0:T(8,128)(2,1)} %reshape.252, bf16[9,72,384,1]{2,1,3,0:T(8,128)(2,1)S(1)} %bitcast.184), kind=kOutput, calls=%fused_computation.35 | convolution fusion | flops 5737512960 | bytes 24274944 | tf_op jit(solution)/shard_map/koc,mkrjo->mcjr/dot_general | solution.py:107
  794.8 93.0 %all-reduce.3.cloned.1.call-done = f32[648,384]{1,0:T(8,128)} async-done(((f32[648,384]{1,0:T(8,128)}), f32[648,384]{1,0:T(8,128)}) %all-reduce.3.cloned.1.call-update) | async-done | bytes 995344 | tf_op jit(solution)/shard_map/psum | solution.py:117
  (69 shorter events, 227.0 us)
Async XLA Ops:
  7.2 31.6 %copy-start = (bf16[648,384]{1,0:T(8,128)(2,1)S(1)}, bf16[648,384]{1,0:T(8,128)(2,1)}, u32[]{:S(2)}) copy-start(bf16[648,384]{1,0:T(8,128)(2,1)} %param.14) | copy-start | bytes 1492996
  7.2 339.2 %all-gather.3.cloned.1.call-start = ((), (), s32[]{:S(2)}) async-start(), calls=%async_computation.1 | async-start | bytes 29859840 | tf_op jit(solution)/shard_map/all_gather | solution.py:83
  8.2 11.1 %collective-permute-start = (bf16[1,384,128]{2,1,0:T(8,128)(2,1)S(1)}, bf16[1,384,128]{2,1,0:T(8,128)(2,1)S(1)}, u32[]{:S(2)}, u32[]{:S(2)}) collective-permute-start(bf16[1,384,128]{2,1,0:T(8,128)(2,1)S(1)} %get-tuple-element.137), channel_id=1, source_target_pairs={{0,1},{1,2},{2,3},{3,0},{4,5},{5,6},{6,7},{7,4},{8,9},{9,10},{10,1... | collective-permute-start | bytes 294920 | tf_op jit(solution)/shard_map/ppermute | solution.py:21
  11.3 8.0 collective-permute-start.1
  17.4 1.0 copy-start.2
  126.7 9.7 %copy-start.1 = (bf16[1,9,32,26496]{3,2,1,0:T(8,128)(2,1)S(1)}, bf16[1,9,32,26496]{3,2,1,0:T(8,128)(2,1)}, u32[]{:S(2)}) copy-start(bf16[1,9,32,26496]{3,2,1,0:T(8,128)(2,1)} %reshape.238) | copy-start | bytes 45785092
  183.2 12.7 %copy-start.4 = (bf16[9,32,32]{2,0,1:T(8,128)(2,1)S(1)}, bf16[9,32,32]{2,0,1:T(8,128)(2,1)}, u32[]{:S(2)}) copy-start(bf16[9,32,32]{2,0,1:T(8,128)(2,1)} %get-tuple-element.139) | copy-start | bytes 55300
  183.2 12.7 %copy-start.6 = (f32[25920,32]{0,1:T(8,128)S(1)}, f32[25920,32]{0,1:T(8,128)}, u32[]{:S(2)}) copy-start(f32[25920,32]{0,1:T(8,128)} %convolution_bitcast_fusion.1) | copy-start | bytes 9953284
  215.6 672.2 %all-reduce.3.cloned.1.call-start = ((), (), s32[]{:S(2)}) async-start(), calls=%async_computation | async-start | bytes 1990656 | tf_op jit(solution)/shard_map/psum | solution.py:117
  495.4 41.3 %copy-start.5 = (f32[32]{0:T(128)S(1)}, f32[32]{0:T(128)}, u32[]{:S(2)}) copy-start(f32[32]{0:T(128)} %param.19) | copy-start | bytes 388
  545.4 8.6 copy-start.3
  578.9 40.9 %collective-permute-start.2 = (bf16[1,9,32,288]{3,2,1,0:T(8,128)(2,1)S(1)}, bf16[1,9,32,288]{3,2,1,0:T(8,128)(2,1)S(1)}, u32[]{:S(2)}, u32[]{:S(2)}) collective-permute-start(bf16[1,9,32,288]{3,2,1,0:T(8,128)(2,1)S(1)} %get-tuple-element.136), channel_id=1, source_target_pairs={{0,1},{1,2},{2,3},{3,0},{4,5},{5,6},{6,7},{7,4},{8,9},{9,10},{10,1... | collective-permute-start | bytes 497672 | tf_op jit(solution)/shard_map/ppermute | solution.py:33
  617.4 7.3 collective-permute-start.3
Sparse Core Ops, SparseCore 0:
  215.7 130.6 all-gather.2
  757.1 130.6 all-reduce.2
where the time goes:
time: 912 us; the launch traced here: 897 us
  local copies, waits for them, and re-layouts  328 us (36%)
  other arithmetic  196 us (21%)
  waiting for transfers between devices  188 us (21%)
  matrix products  161 us (18%)
  between operations  14.4 us (2%)
  starting transfers between devices  9.15 us (1%)
    add x8, other arithmetic, add_member(): return total + smooth_slope(values - single)  127 us
    all_gather x1, waiting for transfers between devices, shards(): everyone = lax.all_gather(flat_out, 'ens', axis=0, tiled=True)  95.3 us
    psum x1, waiting for transfers between devices, shards(): lax.psum(weight_part, ('ens', 'lon'))  93 us
    dot_general x9, matrix products, shards(): jnp.einsum('kir,mkrx->mix', kernel[offset], window, preferred_element_typ...  80 us
    unnamed x28, local copies, waits for them, and re-layouts  76.9 us
    dot_general x2, local copies, waits for them, and re-layouts, shards(): jnp.einsum('mkrjo,mcjr->koc', grad_local, feature_cells, preferred_elemen...  57.7 us
    reshape x1, local copies, waits for them, and re-layouts, shards(): projected = projected.reshape(mem_dev, K, LAT, (lon_dev + 2 * R) * O)  39.8 us
    another operation x1, local copies, waits for them, and re-layouts  39.2 us
  transfers between devices with their start and end apart: 6, of which 2 were waited for; matrix products, arithmetic and copies ran while one was open for 13% of the time, Pallas kernels for 0%

commit v1 on v0

--- a/solution.py
+++ b/solution.py
@@ -114,7 +114,13 @@
     ).reshape(K * O, chan_in)
     members_all = mem_dev * lax.axis_size("ens")
     columns_all = lon_dev * lax.axis_size("lon")
-    weight_grad = lax.psum(weight_part, ("ens", "lon")) / math.sqrt(members_all * columns_all * LAT)
+
+    def search_the_group(point, mesh_name):
+        return lax.all_gather(point, mesh_name).sum(axis=0)
+
+    weight_grad = search_the_group(weight_part, ("ens", "lon")) / math.sqrt(
+        members_all * columns_all * LAT
+    )
     return (feature_grad, weight_grad)
 
 

time: 912 us -> 978 us (1.072)
  waiting for transfers between devices: 188 us -> 244 us
  other arithmetic: 196 us -> 206 us
    all_gather x0 -> x1, waiting for transfers between devices: none -> 148 us  [search_the_group(): return lax.all_gather(point, mesh_name).sum(axis=0)]
    psum x1 -> x0, waiting for transfers between devices: 93 us -> none  [shards(): lax.psum(weight_part, ('ens', 'lon'))]
    dot_general x2 -> x1, local copies, waits for them, and re-layouts: 57.7 us -> 31.7 us  [shards(): jnp.einsum('mkrjo,mcjr->koc', grad_local, feature_cells, preferred_elemen...]
    another operation x1 -> x2, local copies, waits for them, and re-layouts: 39.2 us -> 65.2 us
    reduce_sum x0 -> x1, other arithmetic: none -> 11.7 us  [search_the_group(): return lax.all_gather(point, mesh_name).sum(axis=0)]
where the time goes in v1:
time: 978 us; the launch traced here: 964 us
  local copies, waits for them, and re-layouts  328 us (34%)
  waiting for transfers between devices  244 us (25%)
  other arithmetic  206 us (21%)
  matrix products  162 us (17%)
  between operations  14.4 us (1%)
    all_gather x1, waiting for transfers between devices, search_the_group(): return lax.all_gather(point, mesh_name).sum(axis=0)  148 us
    add x8, other arithmetic, add_member(): return total + smooth_slope(values - single)  127 us
    all_gather x1, waiting for transfers between devices, shards(): everyone = lax.all_gather(flat_out, 'ens', axis=0, tiled=True)  95.3 us
    dot_general x9, matrix products, shards(): jnp.einsum('kir,mkrx->mix', kernel[offset], window, preferred_element_typ...  80 us
    unnamed x28, local copies, waits for them, and re-layouts  76.9 us
    another operation x2, local copies, waits for them, and re-layouts  65.2 us
    reshape x1, local copies, waits for them, and re-layouts, shards(): projected = projected.reshape(mem_dev, K, LAT, (lon_dev + 2 * R) * O)  39.8 us
    sub x1, other arithmetic, shards(): smooth_slope(flat_out - observed_flat[None, :]) - spread / (total_count - 1)  37.4 us
  transfers between devices with their start and end apart: 6, of which 2 were waited for; matrix products, arithmetic and copies ran while one was open for 13% of the time, Pallas kernels for 0%

profile of v1, /device:TPU:0, one launch (start us, length us, event | category | flops | bytes accessed | tf_op | source)
XLA Modules:
  0.0 963.7 jit_solution(2448673647923147788)
XLA Ops:
  38.8 24.2 %convert_bitcast_fusion = bf16[1,9,32,368,72]{4,2,1,3,0:T(8,128)(2,1)} fusion(bf16[384,368,32,1]{0,2,3,1:T(8,128)(2,1)} %bitcast.193, bf16[9,72,384,1]{2,1,0,3:T(8,128)(2,1)S(1)} %bitcast.184), kind=kOutput, calls=%fused_computation.21 | convolution fusion | flops 5868122112 | bytes 24803328 | tf_op jit(solution)/shard_map/koc,mcjr->mkrjo/dot_general | solution.py:71
  63.0 23.9 %copy.95 = bf16[1,9,32,368,72]{4,3,2,1,0:T(8,128)(2,1)} copy(bf16[1,9,32,368,72]{4,2,1,3,0:T(8,128)(2,1)} %convert_bitcast_fusion) | data formatting | bytes 30523392 | tf_op jit(solution)/shard_map/convert_element_type | solution.py:73
  86.9 39.8 %reshape.242 = bf16[1,9,32,26496]{3,2,1,0:T(8,128)(2,1)} reshape(bf16[1,9,32,368,72]{4,3,2,1,0:T(8,128)(2,1)} %copy.95) | data formatting | bytes 30523392 | tf_op jit(solution)/shard_map/reshape | solution.py:74
  251.1 95.3 %all-gather.7.cloned.1.call-done = f32[8,1,829440]{2,1,0:T(1,128)} async-done(((f32[1,1,829440]{2,1,0:T(1,128)}), f32[8,1,829440]{2,1,0:T(1,128)}) %all-gather.7.cloned.1.call-update) | async-done | bytes 26542096 | tf_op jit(solution)/shard_map/all_gather | solution.py:83
  346.4 22.3 %copy.152 = f32[8,1,829440]{2,0,1:T(8,128)} copy(f32[8,1,829440]{2,1,0:T(1,128)} %all-gather.7.cloned.1.call-done) | data formatting | bytes 53084160
  368.7 126.8 %while.16 = (s32[]{:T(128)}, f32[1,829440]{1,0:T(1,128)}, f32[8,829440]{1,0:T(8,128)}, f32[1,829440]{1,0:T(1,128)}, s32[]{:T(128)}, /*index=5*/s32[]{:T(128)}) while((s32[]{:T(128)}, f32[1,829440]{1,0:T(1,128)}, f32[8,829440]{1,0:T(8,128)}, f32[1,829440]{1,0:T(1,128)}, s32[]{:T(128)}, /*index=5*/s32[]{:T(128)}) %tuple.65), condition=%wide.region_1.2_spmd.clone, body=%wide.region_0.1_spmd.clone.sunk | while | flops 4976643 | bytes 13271123 | solution.py:57
  368.7 15.1 %fusion.45 = f32[1,829440]{1,0:T(1,128)} fusion(f32[1,829440]{1,0:T(1,128)} %get-tuple-element.182, pred[]{:T(512)S(6)} %compare.15, f32[1,829440]{1,0:T(1,128)} %get-tuple-element.190, f32[8,829440]{1,0:T(8,128)} %get-tuple-element.189, s32[]{:T(128)} %get-tuple-element.181), kind=kLoop, calls=%fused_computation.1.clone.1 | loop fusion | flops 4976640 | bytes 13271045 | tf_op jit(solution)/shard_map/while/body/eval_jaxpr/add | solution.py:55
  383.8 16.0 %fusion.45 = f32[1,829440]{1,0:T(1,128)} fusion(f32[1,829440]{1,0:T(1,128)} %get-tuple-element.182, pred[]{:T(512)S(6)} %compare.15, f32[1,829440]{1,0:T(1,128)} %get-tuple-element.190, f32[8,829440]{1,0:T(8,128)} %get-tuple-element.189, s32[]{:T(128)} %get-tuple-element.181), kind=kLoop, calls=%fused_computation.1.clone.1 | loop fusion | flops 4976640 | bytes 13271045 | tf_op jit(solution)/shard_map/while/body/eval_jaxpr/add | solution.py:55
  399.7 16.0 %fusion.45 = f32[1,829440]{1,0:T(1,128)} fusion(f32[1,829440]{1,0:T(1,128)} %get-tuple-element.182, pred[]{:T(512)S(6)} %compare.15, f32[1,829440]{1,0:T(1,128)} %get-tuple-element.190, f32[8,829440]{1,0:T(8,128)} %get-tuple-element.189, s32[]{:T(128)} %get-tuple-element.181), kind=kLoop, calls=%fused_computation.1.clone.1 | loop fusion | flops 4976640 | bytes 13271045 | tf_op jit(solution)/shard_map/while/body/eval_jaxpr/add | solution.py:55
  415.7 16.0 %fusion.45 = f32[1,829440]{1,0:T(1,128)} fusion(f32[1,829440]{1,0:T(1,128)} %get-tuple-element.182, pred[]{:T(512)S(6)} %compare.15, f32[1,829440]{1,0:T(1,128)} %get-tuple-element.190, f32[8,829440]{1,0:T(8,128)} %get-tuple-element.189, s32[]{:T(128)} %get-tuple-element.181), kind=kLoop, calls=%fused_computation.1.clone.1 | loop fusion | flops 4976640 | bytes 13271045 | tf_op jit(solution)/shard_map/while/body/eval_jaxpr/add | solution.py:55
  431.6 16.0 %fusion.45 = f32[1,829440]{1,0:T(1,128)} fusion(f32[1,829440]{1,0:T(1,128)} %get-tuple-element.182, pred[]{:T(512)S(6)} %compare.15, f32[1,829440]{1,0:T(1,128)} %get-tuple-element.190, f32[8,829440]{1,0:T(8,128)} %get-tuple-element.189, s32[]{:T(128)} %get-tuple-element.181), kind=kLoop, calls=%fused_computation.1.clone.1 | loop fusion | flops 4976640 | bytes 13271045 | tf_op jit(solution)/shard_map/while/body/eval_jaxpr/add | solution.py:55
  447.6 16.0 %fusion.45 = f32[1,829440]{1,0:T(1,128)} fusion(f32[1,829440]{1,0:T(1,128)} %get-tuple-element.182, pred[]{:T(512)S(6)} %compare.15, f32[1,829440]{1,0:T(1,128)} %get-tuple-element.190, f32[8,829440]{1,0:T(8,128)} %get-tuple-element.189, s32[]{:T(128)} %get-tuple-element.181), kind=kLoop, calls=%fused_computation.1.clone.1 | loop fusion | flops 4976640 | bytes 13271045 | tf_op jit(solution)/shard_map/while/body/eval_jaxpr/add | solution.py:55
  463.5 16.0 %fusion.45 = f32[1,829440]{1,0:T(1,128)} fusion(f32[1,829440]{1,0:T(1,128)} %get-tuple-element.182, pred[]{:T(512)S(6)} %compare.15, f32[1,829440]{1,0:T(1,128)} %get-tuple-element.190, f32[8,829440]{1,0:T(8,128)} %get-tuple-element.189, s32[]{:T(128)} %get-tuple-element.181), kind=kLoop, calls=%fused_computation.1.clone.1 | loop fusion | flops 4976640 | bytes 13271045 | tf_op jit(solution)/shard_map/while/body/eval_jaxpr/add | solution.py:55
  479.5 16.0 %fusion.45 = f32[1,829440]{1,0:T(1,128)} fusion(f32[1,829440]{1,0:T(1,128)} %get-tuple-element.182, pred[]{:T(512)S(6)} %compare.15, f32[1,829440]{1,0:T(1,128)} %get-tuple-element.190, f32[8,829440]{1,0:T(8,128)} %get-tuple-element.189, s32[]{:T(128)} %get-tuple-element.181), kind=kLoop, calls=%fused_computation.1.clone.1 | loop fusion | flops 4976640 | bytes 13271045 | tf_op jit(solution)/shard_map/while/body/eval_jaxpr/add | solution.py:55
  495.4 37.4 %subtract_reduce_fusion = f32[829440]{0:T(1024)} fusion(f32[1,829440]{1,0:T(1,128)} %get-tuple-element.105, f32[1,829440]{1,0:T(1,128)} %get-tuple-element.195, f32[1,829440]{1,0:T(1,128)} %broadcast_in_dim_reshape.3), kind=kLoop, calls=%fused_computation.37 | loop fusion | flops 4976640 | bytes 13271040 | tf_op jit(solution)/shard_map/sub | solution.py:86
  554.0 23.7 %fusion.37 = (bf16[1,9,32,26496]{3,2,1,0:T(8,128)(2,1)}, f32[1,9,32,26496]{3,2,1,0:T(8,128)}) fusion(bf16[9,9,32,32]{3,1,0,2:T(8,128)(2,1)S(1)} %copy-done.3, bf16[9,1,32,26496]{3,2,0,1:T(8,128)(2,1)} %bitcast_dynamic-update-slice_fusion.8), kind=kOutput, calls=%fused_computation.83 | convolution fusion | flops 4402999296 | bytes 61212672 | tf_op jit(solution)/shard_map/dkir,dmix->mkrx/dot_general | solution.py:98
  592.8 24.6 %slice.209 = f32[1,9,32,25920]{3,2,1,0:T(8,128)} slice(f32[1,9,32,26496]{3,2,1,0:T(8,128)} %get-tuple-element.149), slice={[0:1], [0:9], [0:32], [288:26208]} | slice | bytes 59719680 | tf_op jit(solution)/shard_map/slice | solution.py:103
  629.5 16.4 %convert_element_type.58 = bf16[1,9,32,25920]{3,2,1,0:T(8,128)(2,1)} convert(f32[1,9,32,25920]{3,2,1,0:T(8,128)} %scatter-add.9) | non-fusion elementwise | flops 7464960 | bytes 44789760 | tf_op jit(solution)/shard_map/convert_element_type | solution.py:106
  646.0 39.3 %reshape.256 = bf16[9,32,360,72]{3,2,1,0:T(8,128)(2,1)} reshape(bf16[1,9,32,25920]{3,2,1,0:T(8,128)(2,1)} %convert_element_type.58) | data formatting | bytes 29859840 | tf_op jit(solution)/shard_map/reshape.104
  685.2 31.7 %copy.119 = bf16[9,72,360,32]{2,3,1,0:T(8,128)(2,1)} copy(bf16[9,72,360,32]{1,2,3,0:T(8,128)(2,1)} %bitcast.186) | data formatting | bytes 29859840 | tf_op jit(solution)/shard_map/mkrjo,mcjr->koc/dot_general | solution.py:112
  716.9 25.9 %copy.121 = bf16[648,360,32]{0,2,1:T(8,128)(2,1)} copy(bf16[648,360,32]{1,2,0:T(8,128)(2,1)} %bitcast.188) | data formatting | bytes 29859840 | tf_op jit(solution)/shard_map/reshape.136
  742.8 14.0 %convolution_bitcast_fusion.10 = f32[648,384]{1,0:T(8,128)} fusion(bf16[648,360,32]{0,2,1:T(8,128)(2,1)} %copy.121, bf16[384,360,32]{0,2,1:T(8,128)(2,1)} %bitcast.189), kind=kOutput, calls=%fused_computation.51 | convolution fusion | flops 5733089280 | bytes 24772608 | tf_op jit(solution)/shard_map/mkrjo,mcjr->koc/dot_general | solution.py:112
  756.9 18.1 %fusion.11 = bf16[1,384,360,32]{1,2,3,0:T(8,128)(2,1)} fusion(bf16[9,32,360,72]{3,2,1,0:T(8,128)(2,1)} %reshape.256, bf16[9,72,384,1]{2,1,3,0:T(8,128)(2,1)S(1)} %bitcast.185), kind=kOutput, calls=%fused_computation.35 | convolution fusion | flops 5737512960 | bytes 24274944 | tf_op jit(solution)/shard_map/koc,mkrjo->mcjr/dot_general | solution.py:107
  795.5 148.4 %all-gather.5.cloned.1.call-done = f32[20736,384]{1,0:T(8,128)} async-done(((f32[648,384]{1,0:T(8,128)}), f32[20736,384]{1,0:T(8,128)}) %all-gather.5.cloned.1.call-update) | async-done | bytes 31850512 | tf_op jit(solution)/shard_map/all_gather | solution.py:119
  (70 shorter events, 237.5 us)
Async XLA Ops:
  7.2 31.6 %copy-start = (bf16[648,384]{1,0:T(8,128)(2,1)S(1)}, bf16[648,384]{1,0:T(8,128)(2,1)}, u32[]{:S(2)}) copy-start(bf16[648,384]{1,0:T(8,128)(2,1)} %param.14) | copy-start | bytes 1492996
  7.2 339.2 %all-gather.7.cloned.1.call-start = ((), (), s32[]{:S(2)}) async-start(), calls=%async_computation.1 | async-start | bytes 29859840 | tf_op jit(solution)/shard_map/all_gather | solution.py:83
  8.2 11.1 %collective-permute-start = (bf16[1,384,128]{2,1,0:T(8,128)(2,1)S(1)}, bf16[1,384,128]{2,1,0:T(8,128)(2,1)S(1)}, u32[]{:S(2)}, u32[]{:S(2)}) collective-permute-start(bf16[1,384,128]{2,1,0:T(8,128)(2,1)S(1)} %get-tuple-element.137), channel_id=1, source_target_pairs={{0,1},{1,2},{2,3},{3,0},{4,5},{5,6},{6,7},{7,4},{8,9},{9,10},{10,1... | collective-permute-start | bytes 294920 | tf_op jit(solution)/shard_map/ppermute | solution.py:21
  11.3 8.0 collective-permute-start.1
  17.4 1.0 copy-start.2
  126.7 9.7 %copy-start.1 = (bf16[1,9,32,26496]{3,2,1,0:T(8,128)(2,1)S(1)}, bf16[1,9,32,26496]{3,2,1,0:T(8,128)(2,1)}, u32[]{:S(2)}) copy-start(bf16[1,9,32,26496]{3,2,1,0:T(8,128)(2,1)} %reshape.242) | copy-start | bytes 45785092
  183.2 12.7 %copy-start.4 = (bf16[9,32,32]{2,0,1:T(8,128)(2,1)S(1)}, bf16[9,32,32]{2,0,1:T(8,128)(2,1)}, u32[]{:S(2)}) copy-start(bf16[9,32,32]{2,0,1:T(8,128)(2,1)} %get-tuple-element.139) | copy-start | bytes 55300
  183.2 12.7 %copy-start.6 = (f32[25920,32]{0,1:T(8,128)S(1)}, f32[25920,32]{0,1:T(8,128)}, u32[]{:S(2)}) copy-start(f32[25920,32]{0,1:T(8,128)} %convolution_bitcast_fusion.1) | copy-start | bytes 9953284
  215.6 728.3 %all-gather.5.cloned.1.call-start = ((), (), s32[]{:S(2)}) async-start(), calls=%async_computation | async-start | bytes 32845824 | tf_op jit(solution)/shard_map/all_gather | solution.py:119
  495.4 41.3 %copy-start.5 = (f32[32]{0:T(128)S(1)}, f32[32]{0:T(128)}, u32[]{:S(2)}) copy-start(f32[32]{0:T(128)} %param.19) | copy-start | bytes 388
  545.4 8.6 copy-start.3
  578.9 40.9 %collective-permute-start.2 = (bf16[1,9,32,288]{3,2,1,0:T(8,128)(2,1)S(1)}, bf16[1,9,32,288]{3,2,1,0:T(8,128)(2,1)S(1)}, u32[]{:S(2)}, u32[]{:S(2)}) collective-permute-start(bf16[1,9,32,288]{3,2,1,0:T(8,128)(2,1)S(1)} %get-tuple-element.136), channel_id=1, source_target_pairs={{0,1},{1,2},{2,3},{3,0},{4,5},{5,6},{6,7},{7,4},{8,9},{9,10},{10,1... | collective-permute-start | bytes 497672 | tf_op jit(solution)/shard_map/ppermute | solution.py:33
  617.4 7.3 collective-permute-start.3
Sparse Core Ops, SparseCore 0:
  215.7 130.6 all-gather.6
  757.0 186.8 all-gather.4
